TPU v7x, 256 devices: a whole 4x4x8 slice. The times are simulated.
256 devices in a mesh: seq: 32 (over x_lo, z, core), wt: 8 (over y, x_hi).
Axes of the slice: x: 4 (x_hi: 2, x_lo: 2; x = x_hi * 2 + x_lo), y: 4, z: 8, core: 2. Of those that a mesh axis runs over, the one named last changes fastest.
Arguments:
- tokens: int32 [8, 4096], P('wt', 'seq'), may hold values from 0 to 511
- embed_table: bfloat16 [512, 8192], P(None, 'wt'), may hold values from -8 to 8
- norm_gain: bfloat16 [8192], P('wt'), may hold values from 0.099609375 to 1.8984375
- w_in: bfloat16 [8192, 3, 4096], P('wt', None, 'seq'), may hold values from -0.0625 to 0.0625
- short_taps: bfloat16 [3, 3, 4096], P(None, None, 'seq'), may hold values from -3 to 3
- filters: bfloat16 [256, 128], P('seq'), may hold values from -2 to 2
- w_out: bfloat16 [8192, 4096], P('wt'), may hold values from -0.09375 to 0.09375
Outputs:
- block_out: bfloat16 [8, 4096, 8192], P(None, 'seq', 'wt')
All inputs are finite; a program needn't handle non-finite values.
Results may differ from a plain program's by a relative error of at most 0.0088.
Values may be sent and summed in bfloat16 or wider, within the bound.
A program may use at most 128 MiB of HBM per device.

v0:
```python
import jax
import jax.numpy as jnp
from jax import lax
from jax.sharding import PartitionSpec as P


def shifted(shard, axis, by):
    size = lax.axis_size(axis)
    pairs = [(i, i + by) for i in range(size) if 0 <= i + by < size]
    return lax.ppermute(shard, axis, pairs)


def causal_pair(filter_vals):
    tap_count = filter_vals.shape[1]
    group_count = filter_vals.shape[0]
    tiled_taps = jnp.tile(filter_vals, (1, 2 * tap_count - 1)).reshape(
        group_count, tap_count, 2 * tap_count - 1
    )[:, :, :tap_count]
    circulant = jnp.swapaxes(tiled_taps, 1, 2)
    row_pos = lax.broadcasted_iota(jnp.int32, (tap_count, tap_count), 0)
    col_pos = lax.broadcasted_iota(jnp.int32, (tap_count, tap_count), 1)
    lower_mask = (row_pos >= col_pos)[None]
    zero_mat = jnp.zeros_like(circulant)
    return (jnp.where(lower_mask, circulant, zero_mat), jnp.where(lower_mask, zero_mat, circulant))


def short_mix(extended, tap_vals):
    row_count = extended.shape[0] - 2
    ext_vals = extended.astype(jnp.float32)
    return (
        tap_vals[0] * ext_vals[2 : 2 + row_count]
        + tap_vals[1] * ext_vals[1 : 1 + row_count]
        + tap_vals[2] * ext_vals[0:row_count]
    )


def run_filter(extended, lower_mat, upper_mat):
    tap_count = lower_mat.shape[1]
    group_count = lower_mat.shape[0]
    chan_count = extended.shape[1]
    blocks = extended.shape[0] // tap_count
    stacked = extended.reshape(blocks, tap_count, group_count, chan_count // group_count)
    filtered = jnp.einsum(
        "gij,bjgc->bigc", lower_mat, stacked[1:], preferred_element_type=jnp.float32
    )
    filtered = filtered + jnp.einsum(
        "gij,bjgc->bigc", upper_mat, stacked[:-1], preferred_element_type=jnp.float32
    )
    return filtered.reshape((blocks - 1) * tap_count, chan_count)


def local(tokens, embed_table, norm_gain, w_in, short_taps, filters, w_out):
    token_ids = tokens[0]
    own_len = token_ids.shape[0]
    tap_count = filters.shape[1]
    table_vals = embed_table.astype(jnp.float32)
    square_sums = lax.psum(jnp.sum(table_vals * table_vals, axis=1, keepdims=True), "wt")
    feature_count = embed_table.shape[1] * lax.axis_size("wt")
    row_scale = lax.rsqrt(square_sums / feature_count + 1e-06)
    normed = (table_vals * row_scale * norm_gain.astype(jnp.float32)).astype(jnp.bfloat16)
    local_chans = w_in.shape[2]
    w_flat = w_in.reshape(w_in.shape[0], 3 * local_chans)
    vocab_size = embed_table.shape[0]
    partial_sum = jnp.dot(normed, w_flat, preferred_element_type=jnp.float32)
    vocab_flat = lax.psum(partial_sum, "wt").astype(jnp.bfloat16)
    vocab_proj = vocab_flat.reshape(vocab_size, 3, local_chans)
    vocab_all, tap_all, filter_all = (
        lax.all_gather(vocab_proj, "seq", axis=2, tiled=True),
        lax.all_gather(short_taps, "seq", axis=2, tiled=True),
        lax.all_gather(filters, "seq", axis=0, tiled=True),
    )
    projected = jnp.take(vocab_all, token_ids, axis=0)
    edge_prev = shifted(projected[own_len - 2 :], "seq", 1)
    mixture = short_mix(
        jnp.concatenate([edge_prev, projected], axis=0), tap_all.astype(jnp.float32)
    )
    product = (mixture[:, 0] * mixture[:, 2]).astype(jnp.bfloat16)
    tail_prev = shifted(product[own_len - tap_count + 1 :], "seq", 1)
    chan_count = product.shape[1]
    extended = jnp.concatenate(
        [jnp.zeros((1, chan_count), jnp.bfloat16), tail_prev, product], axis=0
    )
    lower_mat, upper_mat = causal_pair(filter_all)
    filtered = run_filter(extended, lower_mat, upper_mat)
    gated = (mixture[:, 1] * filtered).astype(jnp.bfloat16)
    everyone = lax.all_gather(tokens, "wt", axis=0, tiled=True)
    branch = jnp.einsum(
        "knc,dc->knd",
        lax.all_gather(gated[None], "wt", axis=0, tiled=True),
        w_out,
        preferred_element_type=jnp.float32,
    )
    embedded = jnp.take(embed_table, everyone, axis=0)
    return (embedded.astype(jnp.float32) + branch).astype(jnp.bfloat16)


def solution(mesh):
    placed = (
        P("wt", "seq"),
        P(None, "wt"),
        P("wt"),
        P("wt", None, "seq"),
        P(None, None, "seq"),
        P("seq", None),
        P("wt", None),
    )
    return jax.shard_map(
        local, mesh=mesh, in_specs=placed, out_specs=P(None, "seq", "wt"), check_vma=False
    )
```

profile of v0, /device:TPU:1, one launch (start us, length us, event | category | flops | bytes accessed | tf_op | source)
XLA Modules:
  0.0 520.0 jit_solution(13024097358544034017)
XLA Ops:
  9.5 21.6 %psum.14 = f32[512,1]{0,1:T(1,128)S(1)} all-reduce(f32[512,1]{0,1:T(1,128)S(1)} %bitcast.66), channel_id=1, replica_groups=mesh['seq'=32,'wt'=8] {'wt'}, use_global_device_ids=true, to_apply=%region_1.0 | all-reduce | flops 512 | bytes 4096 | tf_op jit(solution)/shard_map/psum | solution.py:57
  33.8 42.2 %all-reduce.2 = bf16[512,384]{1,0:T(8,128)(2,1)S(1)} all-reduce(f32[512,384]{1,0:T(8,128)S(1)} %fusion.12), channel_id=1, replica_groups=mesh['seq'=32,'wt'=8] {'wt'}, use_global_device_ids=true, to_apply=%region_2.0 | all-reduce | flops 196608 | bytes 1179648 | tf_op jit(solution)/shard_map/psum | solution.py:65
  77.3 48.3 %all_gather.16 = bf16[3,3,4096]{2,1,0:T(4,128)(2,1)S(1)} all-gather(bf16[3,3,128]{2,1,0:T(4,128)(2,1)S(1)} %copy-done.2), channel_id=1, replica_groups=mesh['seq'=32,'wt'=8] {'seq'}, dimensions={2}, use_global_device_ids=true | all-gather | bytes 76032 | tf_op jit(solution)/shard_map/all_gather | solution.py:69
  125.7 85.9 %all-gather.4.cloned.1.call-done = bf16[512,3,4096]{2,1,0:T(4,128)(2,1)} async-done(((bf16[512,3,128]{2,1,0:T(4,128)(2,1)}), bf16[512,3,4096]{2,1,0:T(4,128)(2,1)}) %all-gather.4.cloned.1.call-update) | async-done | bytes 12582928 | tf_op jit(solution)/shard_map/all_gather | solution.py:68
  211.6 13.3 %gather_fusion.1 = bf16[128,3,4096]{2,1,0:T(4,128)(2,1)} fusion(bf16[512,3,4096]{2,1,0:T(4,128)(2,1)} %all-gather.4.cloned.1.call-done, s32[1024]{0:T(1024)S(1)} %pad_clamp_fusion), kind=kCustom, calls=%fused_computation.1 | custom fusion | bytes 6291968 | tf_op jit(solution)/shard_map/jit(_take)/gather | solution.py:72
  224.9 4.3 broadcast_select_fusion.2
  233.5 31.3 %all_gather.18 = bf16[256,128]{1,0:T(8,128)(2,1)S(1)} all-gather(bf16[8,128]{1,0:T(8,128)(2,1)S(1)} %copy-done.3), channel_id=1, replica_groups=mesh['seq'=32,'wt'=8] {'seq'}, dimensions={0}, use_global_device_ids=true | all-gather | bytes 67584 | tf_op jit(solution)/shard_map/all_gather | solution.py:70
  264.9 6.0 %tile.8 = bf16[256,255,128]{0,2,1:T(8,128)(2,1)} broadcast(bf16[256,128]{0,1:T(8,128)(2,1)S(1)} %copy.35), dimensions={0,2} | broadcast | bytes 16777216 | tf_op jit(solution)/shard_map/tile | solution.py:16
  270.9 19.0 %tile.9 = bf16[256,128,255]{0,2,1:T(8,128)(2,1)} reshape(bf16[256,255,128]{0,2,1:T(8,128)(2,1)} %tile.8) | data formatting | bytes 33423360 | tf_op jit(solution)/shard_map/tile | solution.py:16
  289.9 4.7 maximum_convert_fusion
  294.6 9.4 %fusion = f32[128,3,4096]{2,1,0:T(4,128)} fusion(f32[130,3,4096]{2,1,0:T(4,128)S(1)} %maximum_convert_fusion, f32[3,4096]{1,0:T(4,128)S(1)} %get-tuple-element.8, f32[3,4096]{1,0:T(4,128)S(1)} %get-tuple-element.9, f32[3,4096]{1,0:T(4,128)S(1)} %get-tuple-element.7), kind=kLoop, calls=%fused_computation.4 | loop fusion | flops 7864320 | bytes 25313280 | tf_op jit(solution)/shard_map/add | solution.py:31
  304.0 9.2 %fusion.7 = bf16[128,1,4096]{2,1,0:T(2,128)(2,1)S(1)} fusion(f32[128,3,4096]{2,1,0:T(4,128)} %fusion), kind=kLoop, calls=%fused_computation.21 | loop fusion | flops 1048576 | bytes 5242880 | tf_op jit(solution)/shard_map/convert_element_type | solution.py:77
  317.4 3.4 collective-permute-start.1
  320.9 6.1 %broadcast_select_fusion = (bf16[256,128,128]{0,1,2:T(8,128)(2,1)}, bf16[256,128,128]{0,1,2:T(8,128)(2,1)}) fusion(pred[128,128]{0,1:T(8,128)(4,1)S(1)} %iota_compare_fusion, bf16[256,128,255]{0,2,1:T(8,128)(2,1)S(1)} %bitcast.57), kind=kLoop, calls=%fused_computation.10 | loop fusion | flops 8388608 | bytes 25182208 | tf_op jit(solution)/shard_map/jit(_where)/select_n | solution.py:24
  327.0 13.5 %copy.36 = bf16[256,128,128]{2,1,0:T(8,128)(2,1)} copy(bf16[256,128,128]{0,1,2:T(8,128)(2,1)} %get-tuple-element.6) | data formatting | bytes 16777216 | tf_op jit(solution)/shard_map/jit(_where)/select_n | solution.py:24
  340.5 13.5 %copy.38 = bf16[256,128,128]{2,1,0:T(8,128)(2,1)} copy(bf16[256,128,128]{0,1,2:T(8,128)(2,1)} %get-tuple-element.5) | data formatting | bytes 16777216 | tf_op jit(solution)/shard_map/jit(_where)/select_n | solution.py:24
  356.6 6.8 %fusion.17 = f32[256,16,128]{2,1,0:T(8,128)S(1)} fusion(bf16[128,256,16]{0,2,1:T(8,128)(2,1)S(1)} %bitcast.59, bf16[256,128,128]{2,1,0:T(8,128)(2,1)} %copy.36), kind=kOutput, calls=%fused_computation.43 | convolution fusion | flops 134217728 | bytes 11534336 | tf_op jit(solution)/shard_map/gij,bjgc->bigc/dot_general | solution.py:43
  365.5 9.2 %convolution_add_fusion = f32[256,16,128]{2,1,0:T(8,128)} fusion(f32[256,16,128]{2,1,0:T(8,128)S(1)} %fusion.17, bf16[128,256,16]{0,2,1:T(8,128)(2,1)S(1)} %bitcast.60, bf16[256,128,128]{2,1,0:T(8,128)(2,1)} %copy.38), kind=kOutput, calls=%fused_computation.25 | convolution fusion | flops 134742016 | bytes 13631488 | tf_op jit(solution)/shard_map/gij,bjgc->bigc/dot_general | solution.py:46
  374.6 4.9 copy.39
  379.5 6.8 %fusion.9 = bf16[1,128,4096]{2,0,1:T(2,128)(2,1)S(1)} fusion(f32[1,128,4096]{2,0,1:T(1,128)S(1)} %copy.39, f32[128,3,4096]{2,1,0:T(4,128)} %fusion), kind=kLoop, calls=%fused_computation.24 | loop fusion | flops 1048576 | bytes 5242880 | tf_op jit(solution)/shard_map/convert_element_type | solution.py:85
  388.5 18.6 %all-gather = s32[8,1,128]{2,1,0:T(1,128)S(1)} all-gather(s32[1,1,128]{2,1,0:T(1,128)S(1)} %bitcast.68), channel_id=1, replica_groups=mesh['seq'=32,'wt'=8] {'wt'}, dimensions={0}, use_global_device_ids=true | all-gather | bytes 4608 | tf_op jit(solution)/shard_map/all_gather | solution.py:86
  407.1 4.1 gather_fusion
  411.2 87.3 %all-gather.6.cloned.1.call-done = bf16[8,128,4096]{2,1,0:T(8,128)(2,1)} async-done(((bf16[1,128,4096]{2,1,0:T(8,128)(2,1)}), bf16[8,128,4096]{2,1,0:T(8,128)(2,1)}) %all-gather.6.cloned.1.call-update) | async-done | bytes 8388624 | tf_op jit(solution)/shard_map/all_gather | solution.py:89
  498.5 14.7 %add_convert_fusion = bf16[8,128,1024]{2,1,0:T(8,128)(2,1)} fusion(bf16[8,128,1024]{2,1,0:T(8,128)(2,1)S(1)} %bitcast.61, pred[8,128]{1,0:T(8,128)(4,1)S(1)} %compare_and_fusion, bf16[8,128,4096]{2,1,0:T(8,128)(2,1)} %all-gather.6.cloned.1.call-done, bf16[1024,4096]{1,0:T(8,128)(2,1)} %param.13), kind=kOutput, calls=%fused_computation.13 | convolution fusion | flops 8594128896 | bytes 20972544 | tf_op jit(solution)/shard_map/knc,dc->knd/dot_general | solution.py:87
  (49 shorter events, 22.5 us)
Async XLA Ops:
  6.5 205.1 %all-gather.4.cloned.1.call-start = ((), (), s32[]{:S(2)}) async-start(), calls=%async_computation | async-start | bytes 17301504 | tf_op jit(solution)/shard_map/all_gather | solution.py:68
  7.9 69.3 %copy-start.2 = (bf16[3,3,128]{2,1,0:T(4,128)(2,1)S(1)}, bf16[3,3,128]{2,1,0:T(4,128)(2,1)}, u32[]{:S(2)}) copy-start(bf16[3,3,128]{2,1,0:T(4,128)(2,1)} %param.11) | copy-start | bytes 6916
  8.0 117.6 %copy-start.4 = (s32[1,128]{1,0:T(1,128)S(1)}, s32[1,128]{1,0:T(1,128)}, u32[]{:S(2)}) copy-start(s32[1,128]{1,0:T(1,128)} %param.7) | copy-start | bytes 1540
  77.2 421.3 %all-gather.6.cloned.1.call-start = ((), (), s32[]{:S(2)}) async-start(), calls=%async_computation.1 | async-start | bytes 9437184 | tf_op jit(solution)/shard_map/all_gather | solution.py:89
  224.9 8.6 %copy-start.3 = (bf16[8,128]{1,0:T(8,128)(2,1)S(1)}, bf16[8,128]{1,0:T(8,128)(2,1)}, u32[]{:S(2)}) copy-start(bf16[8,128]{1,0:T(8,128)(2,1)} %param.12) | copy-start | bytes 6148
  229.2 2.1 copy-start.1
  231.3 58.6 %collective-permute-start = (bf16[2,3,4096]{2,1,0:T(4,128)(2,1)S(1)}, bf16[2,3,4096]{2,1,0:T(4,128)(2,1)S(1)}, u32[]{:S(2)}, u32[]{:S(2)}) collective-permute-start(bf16[2,3,4096]{2,1,0:T(4,128)(2,1)S(1)} %slice.62), channel_id=1, source_target_pairs={{0,8},{8,16},{16,24},{24,32},{32,40},{40,48},{48,56},{56,64},{64,7... | collective-permute-start | bytes 147464 | tf_op jit(solution)/shard_map/ppermute | solution.py:10
  294.6 26.3 %slice-start = ((s8[16777216]{0:T(1024)(128)(4,1)}), s8[4194304]{0:T(1024)(128)(4,1)S(1)}, s32[]{:S(2)}) async-start(s8[16777216]{0:T(1024)(128)(4,1)} %bitcast.56), calls=%async_computation.2 | async-start | bytes 8388608
  294.6 26.2 %slice-start.1 = ((s8[16777216]{0:T(1024)(128)(4,1)}), s8[4194304]{0:T(1024)(128)(4,1)S(1)}, s32[]{:S(2)}) async-start(s8[16777216]{0:T(1024)(128)(4,1)} %bitcast.56), calls=%async_computation.3 | async-start | bytes 8388608
  294.6 26.2 %slice-start.2 = ((s8[16777216]{0:T(1024)(128)(4,1)}), s8[4194304]{0:T(1024)(128)(4,1)S(1)}, s32[]{:S(2)}) async-start(s8[16777216]{0:T(1024)(128)(4,1)} %bitcast.56), calls=%async_computation.4 | async-start | bytes 8388608
  304.0 16.9 %slice-start.3 = ((s8[16777216]{0:T(1024)(128)(4,1)}), s8[4194304]{0:T(1024)(128)(4,1)S(1)}, s32[]{:S(2)}) async-start(s8[16777216]{0:T(1024)(128)(4,1)} %bitcast.56), calls=%async_computation.5 | async-start | bytes 8388608
  317.4 45.9 %collective-permute-start.1 = (bf16[127,4096]{1,0:T(8,128)(2,1)}, bf16[127,4096]{1,0:T(8,128)(2,1)}, u32[]{:S(2)}, u32[]{:S(2)}) collective-permute-start(bf16[127,4096]{1,0:T(8,128)(2,1)} %bitcast.55), channel_id=1, source_target_pairs={{0,8},{8,16},{16,24},{24,32},{32,40},{40,48},{48,56},{56,64},{64,7... | collective-permute-start | bytes 3121160 | tf_op jit(solution)/shard_map/ppermute | solution.py:10
  379.5 27.6 %copy-start = (bf16[512,1024]{1,0:T(8,128)(2,1)S(1)}, bf16[512,1024]{1,0:T(8,128)(2,1)}, u32[]{:S(2)}) copy-start(bf16[512,1024]{1,0:T(8,128)(2,1)} %param.8) | copy-start | bytes 3145732
Sparse Core Ops, SparseCore 0:
  77.3 134.2 all-gather.3
  388.6 109.8 all-gather.5
where the time goes:
time: 522 us; the launch traced here: 520 us
  waiting for transfers between devices  173 us (33%)
  blocking collectives  162 us (31%)
  local copies, waits for them, and re-layouts  90.2 us (17%)
  other arithmetic  42.6 us (8%)
  matrix products  32.6 us (6%)
  between operations  13.7 us (3%)
  starting transfers between devices  5.63 us (1%)
    all_gather x1, waiting for transfers between devices, local(): lax.all_gather(gated[None], 'wt', axis=0, tiled=True)  87.3 us
    all_gather x1, waiting for transfers between devices, local(): lax.all_gather(vocab_proj, 'seq', axis=2, tiled=True)  85.9 us
    all_gather x1, blocking collectives, local(): lax.all_gather(short_taps, 'seq', axis=2, tiled=True)  48.3 us
    psum x1, blocking collectives, local(): vocab_flat = lax.psum(partial_sum, 'wt').astype(jnp.bfloat16)  42.2 us
    all_gather x1, blocking collectives, local(): lax.all_gather(filters, 'seq', axis=0, tiled=True)  31.3 us
    another operation x2, local copies, waits for them, and re-layouts, causal_pair(): jnp.tile(filter_vals, (1, 2 * tap_count - 1))  25 us
    psum x1, blocking collectives, local(): lax.psum(jnp.sum(table_vals * table_vals, axis=1, keepdims=True), 'wt')  21.6 us
    all_gather x1, blocking collectives, local(): everyone = lax.all_gather(tokens, 'wt', axis=0, tiled=True)  18.6 us
  transfers between devices with their start and end apart: 4, of which 2 were waited for; matrix products, arithmetic and copies ran while one was open for 14% of the time, Pallas kernels for 0%

commit v1 on v0

--- a/solution.py
+++ b/solution.py
@@ -65,7 +65,9 @@
     vocab_flat = lax.psum(partial_sum, "wt").astype(jnp.bfloat16)
     vocab_proj = vocab_flat.reshape(vocab_size, 3, local_chans)
     vocab_all, tap_all, filter_all = (
-        lax.all_gather(vocab_proj, "seq", axis=2, tiled=True),
+        jnp.concatenate(
+            lax.all_to_all(jnp.stack([vocab_proj] * lax.axis_size("seq")), "seq", 0, 0), axis=2
+        ),
         lax.all_gather(short_taps, "seq", axis=2, tiled=True),
         lax.all_gather(filters, "seq", axis=0, tiled=True),
     )

time: 522 us -> 750 us (1.44)
  blocking collectives: 162 us -> 415 us
  waiting for transfers between devices: 173 us -> 84.2 us
  local copies, waits for them, and re-layouts: 90.2 us -> 133 us
  starting transfers between devices: 5.63 us -> 25.9 us
    all_gather x1, blocking collectives: 48.3 us -> 305 us  [local(): lax.all_gather(short_taps, 'seq', axis=2, tiled=True)]
    all_gather x1 -> x0, waiting for transfers between devices: 85.9 us -> none  [local(): lax.all_gather(vocab_proj, 'seq', axis=2, tiled=True)]
    reshape x1, local copies, waits for them, and re-layouts: 1.06 us -> 27.5 us  [local(): jnp.concatenate(lax.all_to_all(jnp.stack([vocab_proj] * lax.axis_size('se...]
    all_to_all x0 -> x1, starting transfers between devices: none -> 20.1 us  [local(): lax.all_to_all(jnp.stack([vocab_proj] * lax.axis_size('seq')), 'seq', 0, 0)]
    all_to_all x0 -> x1, local copies, waits for them, and re-layouts: none -> 10.6 us  [local(): lax.all_to_all(jnp.stack([vocab_proj] * lax.axis_size('seq')), 'seq', 0, 0)]
  transfers between devices with their start and end apart: 4 -> 4, of which waited for: 2 -> 1; matrix products, arithmetic and copies ran while one was open for 14% -> 10% of each run, Pallas kernels for 0% -> 0%
where the time goes in v1:
time: 750 us; the launch traced here: 748 us
  blocking collectives  415 us (55%)
  local copies, waits for them, and re-layouts  133 us (18%)
  waiting for transfers between devices  84.2 us (11%)
  other arithmetic  42.7 us (6%)
  matrix products  32.6 us (4%)
  starting transfers between devices  25.9 us (3%)
  between operations  13.7 us (2%)
    all_gather x1, blocking collectives, local(): lax.all_gather(short_taps, 'seq', axis=2, tiled=True)  305 us
    all_gather x1, waiting for transfers between devices, local(): lax.all_gather(gated[None], 'wt', axis=0, tiled=True)  84.2 us
    psum x1, blocking collectives, local(): vocab_flat = lax.psum(partial_sum, 'wt').astype(jnp.bfloat16)  42.2 us
    all_gather x1, blocking collectives, local(): lax.all_gather(filters, 'seq', axis=0, tiled=True)  31.1 us
    reshape x1, local copies, waits for them, and re-layouts, local(): jnp.concatenate(lax.all_to_all(jnp.stack([vocab_proj] * lax.axis_size('se...  27.5 us
    another operation x2, local copies, waits for them, and re-layouts, causal_pair(): jnp.tile(filter_vals, (1, 2 * tap_count - 1))  25 us
    psum x1, blocking collectives, local(): lax.psum(jnp.sum(table_vals * table_vals, axis=1, keepdims=True), 'wt')  21.6 us
    all_to_all x1, starting transfers between devices, local(): lax.all_to_all(jnp.stack([vocab_proj] * lax.axis_size('seq')), 'seq', 0, 0)  20.1 us
  transfers between devices with their start and end apart: 4, of which 1 were waited for; matrix products, arithmetic and copies ran while one was open for 10% of the time, Pallas kernels for 0%

profile of v1, /device:TPU:1, one launch (start us, length us, event | category | flops | bytes accessed | tf_op | source)
XLA Modules:
  0.0 747.5 jit_solution(9348995799365702396)
XLA Ops:
  9.4 21.6 %psum.14 = f32[512,1]{0,1:T(1,128)S(1)} all-reduce(f32[512,1]{0,1:T(1,128)S(1)} %bitcast.70), channel_id=1, replica_groups=mesh['seq'=32,'wt'=8] {'wt'}, use_global_device_ids=true, to_apply=%region_1.0 | all-reduce | flops 512 | bytes 4096 | tf_op jit(solution)/shard_map/psum | solution.py:57
  33.7 42.2 %all-reduce.2 = bf16[512,384]{1,0:T(8,128)(2,1)S(1)} all-reduce(f32[512,384]{1,0:T(8,128)S(1)} %fusion.12), channel_id=1, replica_groups=mesh['seq'=32,'wt'=8] {'wt'}, use_global_device_ids=true, to_apply=%region_2.0 | all-reduce | flops 196608 | bytes 1179648 | tf_op jit(solution)/shard_map/psum | solution.py:65
  76.1 6.0 stack.3
  82.1 20.1 %all-to-all-start = ((bf16[32,512,3,128]{1,3,2,0:T(8,128)(2,1)}), bf16[32,512,3,128]{1,3,2,0:T(8,128)(2,1)}, u32[]{:S(2)}, u32[]{:S(2)}) async-start(bf16[32,512,3,128]{1,3,2,0:T(8,128)(2,1)} %stack.3), calls=%async_computation | async-start | bytes 25165824 | tf_op jit(solution)/shard_map/all_to_all | solution.py:69
  102.3 304.6 %all_gather.13 = bf16[3,3,4096]{2,1,0:T(4,128)(2,1)S(1)} all-gather(bf16[3,3,128]{2,1,0:T(4,128)(2,1)S(1)} %copy-done.2), channel_id=1, replica_groups=mesh['seq'=32,'wt'=8] {'seq'}, dimensions={2}, use_global_device_ids=true | all-gather | bytes 76032 | tf_op jit(solution)/shard_map/all_gather | solution.py:71
  407.0 10.6 %copy.34 = bf16[32,512,3,128]{1,3,0,2:T(8,128)(2,1)} copy(bf16[32,512,3,128]{1,3,2,0:T(8,128)(2,1)} %all-to-all-done) | data formatting | bytes 25165824 | tf_op jit(solution)/shard_map/all_to_all | solution.py:69
  417.6 27.5 %copy.35 = bf16[512,3,4096]{2,1,0:T(4,128)(2,1)} copy(bf16[512,3,4096]{0,2,1:T(8,128)(2,1)} %bitcast.59) | data formatting | bytes 25165824 | tf_op jit(solution)/shard_map/reshape | solution.py:68
  445.1 13.3 %gather_fusion.1 = bf16[128,3,4096]{2,1,0:T(4,128)(2,1)} fusion(bf16[512,3,4096]{2,1,0:T(4,128)(2,1)} %copy.35, s32[1024]{0:T(1024)S(1)} %pad_clamp_fusion), kind=kCustom, calls=%fused_computation.1 | custom fusion | bytes 6291968 | tf_op jit(solution)/shard_map/jit(_take)/gather | solution.py:74
  466.7 31.1 %all_gather.14 = bf16[256,128]{1,0:T(8,128)(2,1)S(1)} all-gather(bf16[8,128]{1,0:T(8,128)(2,1)S(1)} %copy-done.3), channel_id=1, replica_groups=mesh['seq'=32,'wt'=8] {'seq'}, dimensions={0}, use_global_device_ids=true | all-gather | bytes 67584 | tf_op jit(solution)/shard_map/all_gather | solution.py:72
  497.9 5.9 tile.8
  503.8 19.0 %tile.9 = bf16[256,128,255]{0,2,1:T(8,128)(2,1)} reshape(bf16[256,255,128]{0,2,1:T(8,128)(2,1)} %tile.8) | data formatting | bytes 33423360 | tf_op jit(solution)/shard_map/tile | solution.py:16
  522.9 4.7 maximum_convert_fusion
  527.6 9.4 %fusion = f32[128,3,4096]{2,1,0:T(4,128)} fusion(f32[130,3,4096]{2,1,0:T(4,128)S(1)} %maximum_convert_fusion, f32[3,4096]{1,0:T(4,128)S(1)} %get-tuple-element.8, f32[3,4096]{1,0:T(4,128)S(1)} %get-tuple-element.9, f32[3,4096]{1,0:T(4,128)S(1)} %get-tuple-element.7), kind=kLoop, calls=%fused_computation.4 | loop fusion | flops 7864320 | bytes 25313280 | tf_op jit(solution)/shard_map/add | solution.py:31
  537.0 9.2 %fusion.7 = bf16[128,1,4096]{2,1,0:T(2,128)(2,1)S(1)} fusion(f32[128,3,4096]{2,1,0:T(4,128)} %fusion), kind=kLoop, calls=%fused_computation.21 | loop fusion | flops 1048576 | bytes 5242880 | tf_op jit(solution)/shard_map/convert_element_type | solution.py:79
  554.4 6.1 broadcast_select_fusion
  560.5 13.5 %copy.38 = bf16[256,128,128]{2,1,0:T(8,128)(2,1)} copy(bf16[256,128,128]{0,1,2:T(8,128)(2,1)} %get-tuple-element.6) | data formatting | bytes 16777216 | tf_op jit(solution)/shard_map/jit(_where)/select_n | solution.py:24
  574.0 13.5 %copy.40 = bf16[256,128,128]{2,1,0:T(8,128)(2,1)} copy(bf16[256,128,128]{0,1,2:T(8,128)(2,1)} %get-tuple-element.5) | data formatting | bytes 16777216 | tf_op jit(solution)/shard_map/jit(_where)/select_n | solution.py:24
  590.1 6.8 fusion.17
  599.0 9.2 %convolution_add_fusion = f32[256,16,128]{2,1,0:T(8,128)} fusion(f32[256,16,128]{2,1,0:T(8,128)S(1)} %fusion.17, bf16[128,256,16]{0,2,1:T(8,128)(2,1)S(1)} %bitcast.64, bf16[256,128,128]{2,1,0:T(8,128)(2,1)} %copy.40), kind=kOutput, calls=%fused_computation.25 | convolution fusion | flops 134742016 | bytes 13631488 | tf_op jit(solution)/shard_map/gij,bjgc->bigc/dot_general | solution.py:46
  608.2 4.9 copy.41
  613.0 6.8 fusion.9
  622.0 15.7 %all-gather = s32[8,1,128]{2,1,0:T(1,128)S(1)} all-gather(s32[1,1,128]{2,1,0:T(1,128)S(1)} %bitcast.72), channel_id=1, replica_groups=mesh['seq'=32,'wt'=8] {'wt'}, dimensions={0}, use_global_device_ids=true | all-gather | bytes 4608 | tf_op jit(solution)/shard_map/all_gather | solution.py:88
  641.8 84.2 %all-gather.3.cloned.1.call-done = bf16[8,128,4096]{2,1,0:T(8,128)(2,1)} async-done(((bf16[1,128,4096]{2,1,0:T(8,128)(2,1)}), bf16[8,128,4096]{2,1,0:T(8,128)(2,1)}) %all-gather.3.cloned.1.call-update) | async-done | bytes 8388624 | tf_op jit(solution)/shard_map/all_gather | solution.py:91
  726.0 14.7 %add_convert_fusion = bf16[8,128,1024]{2,1,0:T(8,128)(2,1)} fusion(bf16[8,128,1024]{2,1,0:T(8,128)(2,1)S(1)} %bitcast.65, pred[8,128]{1,0:T(8,128)(4,1)S(1)} %compare_and_fusion, bf16[8,128,4096]{2,1,0:T(8,128)(2,1)} %all-gather.3.cloned.1.call-done, bf16[1024,4096]{1,0:T(8,128)(2,1)} %param.13), kind=kOutput, calls=%fused_computation.13 | convolution fusion | flops 8594128896 | bytes 20972544 | tf_op jit(solution)/shard_map/knc,dc->knd/dot_general | solution.py:89
  (50 shorter events, 33.3 us)
Async XLA Ops:
  82.1 20.1 %copy-start.2 = (bf16[3,3,128]{2,1,0:T(4,128)(2,1)S(1)}, bf16[3,3,128]{2,1,0:T(4,128)(2,1)}, u32[]{:S(2)}) copy-start(bf16[3,3,128]{2,1,0:T(4,128)(2,1)} %param.11) | copy-start | bytes 6916
  82.1 324.8 %copy-start.4 = (s32[1,128]{1,0:T(1,128)S(1)}, s32[1,128]{1,0:T(1,128)}, u32[]{:S(2)}) copy-start(s32[1,128]{1,0:T(1,128)} %param.7) | copy-start | bytes 1540
  82.1 324.9 %all-to-all-start = ((bf16[32,512,3,128]{1,3,2,0:T(8,128)(2,1)}), bf16[32,512,3,128]{1,3,2,0:T(8,128)(2,1)}, u32[]{:S(2)}, u32[]{:S(2)}) async-start(bf16[32,512,3,128]{1,3,2,0:T(8,128)(2,1)} %stack.3), calls=%async_computation | async-start | bytes 25165824 | tf_op jit(solution)/shard_map/all_to_all | solution.py:69
  102.2 623.8 %all-gather.3.cloned.1.call-start = ((), (), s32[]{:S(2)}) async-start(), calls=%async_computation.1 | async-start | bytes 9437184 | tf_op jit(solution)/shard_map/all_gather | solution.py:91
  458.4 8.3 %copy-start.3 = (bf16[8,128]{1,0:T(8,128)(2,1)S(1)}, bf16[8,128]{1,0:T(8,128)(2,1)}, u32[]{:S(2)}) copy-start(bf16[8,128]{1,0:T(8,128)(2,1)} %param.12) | copy-start | bytes 6148
  462.7 2.1 copy-start.1
  464.8 58.1 %collective-permute-start = (bf16[2,3,4096]{2,1,0:T(4,128)(2,1)S(1)}, bf16[2,3,4096]{2,1,0:T(4,128)(2,1)S(1)}, u32[]{:S(2)}, u32[]{:S(2)}) collective-permute-start(bf16[2,3,4096]{2,1,0:T(4,128)(2,1)S(1)} %slice.62), channel_id=1, source_target_pairs={{0,8},{8,16},{16,24},{24,32},{32,40},{40,48},{48,56},{56,64},{64,7... | collective-permute-start | bytes 147464 | tf_op jit(solution)/shard_map/ppermute | solution.py:10
  527.5 26.8 %slice-start = ((s8[16777216]{0:T(1024)(128)(4,1)}), s8[4194304]{0:T(1024)(128)(4,1)S(1)}, s32[]{:S(2)}) async-start(s8[16777216]{0:T(1024)(128)(4,1)} %bitcast.60), calls=%async_computation.2 | async-start | bytes 8388608
  527.5 26.8 %slice-start.1 = ((s8[16777216]{0:T(1024)(128)(4,1)}), s8[4194304]{0:T(1024)(128)(4,1)S(1)}, s32[]{:S(2)}) async-start(s8[16777216]{0:T(1024)(128)(4,1)} %bitcast.60), calls=%async_computation.3 | async-start | bytes 8388608
  527.6 26.8 %slice-start.2 = ((s8[16777216]{0:T(1024)(128)(4,1)}), s8[4194304]{0:T(1024)(128)(4,1)S(1)}, s32[]{:S(2)}) async-start(s8[16777216]{0:T(1024)(128)(4,1)} %bitcast.60), calls=%async_computation.4 | async-start | bytes 8388608
  537.0 17.4 %slice-start.3 = ((s8[16777216]{0:T(1024)(128)(4,1)}), s8[4194304]{0:T(1024)(128)(4,1)S(1)}, s32[]{:S(2)}) async-start(s8[16777216]{0:T(1024)(128)(4,1)} %bitcast.60), calls=%async_computation.5 | async-start | bytes 8388608
  550.5 46.4 %collective-permute-start.1 = (bf16[127,4096]{1,0:T(8,128)(2,1)}, bf16[127,4096]{1,0:T(8,128)(2,1)}, u32[]{:S(2)}, u32[]{:S(2)}) collective-permute-start(bf16[127,4096]{1,0:T(8,128)(2,1)} %bitcast.58), channel_id=1, source_target_pairs={{0,8},{8,16},{16,24},{24,32},{32,40},{40,48},{48,56},{56,64},{64,7... | collective-permute-start | bytes 3121160 | tf_op jit(solution)/shard_map/ppermute | solution.py:10
  613.0 24.7 %copy-start = (bf16[512,1024]{1,0:T(8,128)(2,1)S(1)}, bf16[512,1024]{1,0:T(8,128)(2,1)}, u32[]{:S(2)}) copy-start(bf16[512,1024]{1,0:T(8,128)(2,1)} %param.8) | copy-start | bytes 3145732
Sparse Core Ops, SparseCore 0:
  622.1 103.8 all-gather.2
